TPU v7x, 256 devices: a whole 4x4x8 slice. The times are simulated.
256 devices in a mesh: layer: 8 (over y, core), blk: 32 (over x, z).
Axes of the slice: x: 4, y: 4, z: 8, core: 2. Of those that a mesh axis runs over, the one named last changes fastest.
Arguments:
- source: bfloat16 [8, 2, 128, 32768], P('layer', None, None, 'blk'), may hold values from -6 to 6
- tile_data: bfloat16 [8, 192, 2, 512, 512], P('layer', 'blk'), may hold values from -0.078125 to 0.078125
- tile_rows: int32 [8, 192], P('layer', 'blk'), may hold values from 0 to 63, as said below
- tile_cols: int32 [8, 192], P('layer', 'blk'), may hold values from 0 to 63, as said below
- tile_count: int32 [8, 32], P('layer', 'blk'), may hold values from 4 to 6, as said below
Outputs:
- down_trace: bfloat16 [8, 2, 128, 32768], P('layer', None, None, 'blk')
- up_trace: bfloat16 [8, 2, 128, 32768], P('layer', None, None, 'blk')
Inputs may be any that keep to these rules, and one draw needn't show every extreme that they name: `tile_rows`: every slot of row range g (slots g*6 to (g+1)*6 - 1) has its row block in g*2 to (g+1)*2 - 1; the live slots of one range hold distinct tiles in shuffled order, among them the diagonal tile of each of its row blocks, and the tile one block left of its first row block and one block right of its last where those exist. Slots that are not live also hold valid indices. `tile_cols`: every slot's column block lies within 2 blocks of its row block, inside the grid. `tile_count`: in every section some row range has all 6 slots live.
All inputs are finite; a program needn't handle non-finite values.
Results may differ from a plain program's by a relative error of at most 0.01.
Values may be sent and summed in bfloat16 or wider, within the bound.
No kernel may reach another device: no remote copies, remote signals or barrier semaphores. Data moves between devices by JAX's collectives and lax.ppermute only.
A program may use at most 64 MiB of HBM per device.

v0:
```python
import jax
import jax.numpy as jnp
from jax import lax
from jax.sharding import PartitionSpec as P

BATCHES = 2
BAND = 2


def padded(shard, sides, width):
    for axis, dim in sides:
        devices, length = (lax.axis_size(axis), shard.shape[dim])
        up = [(i, (i + 1) % devices) for i in range(devices - 1)]
        down = [(j, i) for i, j in up]
        last = lax.slice_in_dim(shard, length - width, length, axis=dim)
        initial = lax.slice_in_dim(shard, 0, width, axis=dim)
        before = lax.ppermute(last, axis, up)
        after = lax.ppermute(initial, axis, down)
        shard = jnp.concatenate([before, shard, after], axis=dim)
    return shard


def from_behind(block, axis, distance):
    devices = range(lax.axis_size(axis))
    route = [(i - distance, i) for i in devices if i - distance in devices]
    return lax.ppermute(block, axis, route)


def complex_apply(segment, matrix, contract):
    halves = segment.shape[1]
    flattened = segment.reshape(2 * halves, segment.shape[2])
    numbers = (((1,), (contract,)), ((), ()))
    with_real = lax.dot_general(flattened, matrix[0], numbers, preferred_element_type=jnp.float32)
    with_imag = lax.dot_general(flattened, matrix[1], numbers, preferred_element_type=jnp.float32)
    return jnp.stack(
        (with_real[:halves] - with_imag[halves:], with_imag[:halves] + with_real[halves:])
    )


def on_device(source, tile_data, tile_rows, tile_cols, tile_count):
    layers = lax.axis_size("layer")
    layer_index = lax.axis_index("layer")
    tile_size = tile_data.shape[3]
    rows_dev = source.shape[3]
    all_columns = source.shape[2]
    margin = BAND * tile_size
    first_block = lax.axis_index("blk") * (rows_dev // tile_size)
    batch_count = BATCHES
    columns = all_columns // batch_count
    live_count = tile_count[0, 0]
    row_start = (tile_rows[0] - first_block) * tile_size
    col_start = (tile_cols[0] - first_block) * tile_size + margin
    local_tiles = tile_data[0]
    sources = source[0]
    part_shape = (2, columns, rows_dev)
    step_count = layers + batch_count - 1

    def down_step(step_index, state_pair):
        incoming, collected = state_pair
        batch_index = step_index - layer_index
        active = (batch_index >= 0) & (batch_index < batch_count)
        offset = jnp.clip(batch_index, 0, batch_count - 1) * columns
        present = lax.dynamic_slice_in_dim(sources, offset, columns, 1)
        current = (present.astype(jnp.float32) + incoming.astype(jnp.float32)).astype(jnp.bfloat16)
        earlier = lax.dynamic_slice_in_dim(collected, offset, columns, 1)
        collected = lax.dynamic_update_slice_in_dim(
            collected, jnp.where(active, current, earlier), offset, 1
        )
        extended = padded(current, (("blk", 2),), margin)

        def down_add_tile(slot_index, summed):
            segment = lax.dynamic_slice_in_dim(extended, col_start[slot_index], tile_size, 2)
            matrix = lax.dynamic_index_in_dim(local_tiles, slot_index, 0, keepdims=False)
            product = complex_apply(segment, matrix, 1)
            target = lax.dynamic_slice_in_dim(summed, row_start[slot_index], tile_size, 2)
            return lax.dynamic_update_slice_in_dim(
                summed, target + product, row_start[slot_index], 2
            )

        forward = lax.fori_loop(
            0, jnp.where(active, live_count, 0), down_add_tile, jnp.zeros(part_shape, jnp.float32)
        )
        incoming = from_behind(forward.astype(jnp.bfloat16), "layer", 1)
        return (incoming, collected)

    empty_part = jnp.zeros(part_shape, jnp.bfloat16)
    down_trace = lax.fori_loop(0, step_count, down_step, (empty_part, jnp.zeros_like(sources)))[1]

    def up_step(step_index, state_pair):
        incoming, collected = state_pair
        batch_index = step_index - (layers - 1 - layer_index)
        active = (batch_index >= 0) & (batch_index < batch_count)
        offset = jnp.clip(batch_index, 0, batch_count - 1) * columns
        present = lax.dynamic_slice_in_dim(down_trace, offset, columns, 1)
        current = (present.astype(jnp.float32) + incoming.astype(jnp.float32)).astype(jnp.bfloat16)
        earlier = lax.dynamic_slice_in_dim(collected, offset, columns, 1)
        collected = lax.dynamic_update_slice_in_dim(
            collected, jnp.where(active, current, earlier), offset, 1
        )

        def up_add_tile(slot_index, summed):
            segment = lax.dynamic_slice_in_dim(current, row_start[slot_index], tile_size, 2)
            matrix = lax.dynamic_index_in_dim(local_tiles, slot_index, 0, keepdims=False)
            product = complex_apply(segment, matrix, 0)
            target = lax.dynamic_slice_in_dim(summed, col_start[slot_index], tile_size, 2)
            return lax.dynamic_update_slice_in_dim(
                summed, target + product, col_start[slot_index], 2
            )

        extended = lax.fori_loop(
            0,
            jnp.where(active, live_count, 0),
            up_add_tile,
            jnp.zeros((2, columns, rows_dev + 2 * margin), jnp.float32),
        )
        lower_rim = extended[:, :, :margin].astype(jnp.bfloat16)
        upper_rim = extended[:, :, margin + rows_dev :].astype(jnp.bfloat16)
        from_above = from_behind(lower_rim, "blk", -1)
        from_below = from_behind(upper_rim, "blk", 1)
        backward = extended[:, :, margin : margin + rows_dev]
        backward = backward + from_below.astype(jnp.float32)
        backward = backward + from_above.astype(jnp.float32)
        incoming = from_behind(backward.astype(jnp.bfloat16), "layer", -1)
        return (incoming, collected)

    up_trace = lax.fori_loop(0, step_count, up_step, (empty_part, jnp.zeros_like(sources)))[1]
    return (down_trace[None], up_trace[None])


def solution(mesh):
    in_specs = (
        P("layer", None, None, "blk"),
        P("layer", "blk", None, None, None),
        P("layer", "blk"),
        P("layer", "blk"),
        P("layer", "blk"),
    )
    out_specs = (P("layer", None, None, "blk"), P("layer", None, None, "blk"))
    return jax.shard_map(
        on_device, mesh=mesh, in_specs=in_specs, out_specs=out_specs, check_vma=False
    )
```

profile of v0, /device:TPU:7, one launch (start us, length us, event | category | flops | bytes accessed | tf_op | source)
XLA Modules:
  0.0 1273.1 jit_solution(12537953310574723991)
XLA Ops:
  1.4 484.2 %while.83 = (s32[]{:T(128)}, bf16[2,64,1024]{2,1,0:T(8,128)(2,1)S(1)}, bf16[2,128,1024]{2,1,0:T(8,128)(2,1)S(1)}, s32[]{:T(128)}, s32[]{:T(128)}, /*index=5*/bf1...) while((s32[]{:T(128)}, ...), condition=%wide.region_3.4_spmd, body=%wide.region_0.3_spmd.sunk | while | flops 137560080 | bytes 11535177 | solution.py:87
  6.1 6.1 collective-permute-start.3
  22.0 52.5 %collective-permute-done.5 = bf16[2,64,1024]{2,1,0:T(8,128)(2,1)S(1)} collective-permute-done((bf16[2,64,1024]{2,1,0:T(8,128)(2,1)S(1)}, bf16[2,64,1024]{2,1,0:T(8,128)(2,1)S(1)}, u32[]{:S(2)}, u32[]{:S(2)}) %collective-permute-start.5) | collective-permute-done | bytes 262176 | tf_op jit(solution)/shard_map/while/body/eval_jaxpr/ppermute | solution.py:26
  88.4 44.5 %while.86 = (s32[]{:T(128)}, f32[2,64,1024]{2,1,0:T(8,128)S(1)}, s32[]{:T(128)}, s32[6]{0:T(128)S(1)}, s32[6]{0:T(128)S(1)}, /*index=5*/bf16[2,64,3072]{2,1,0:T(...) while((s32[]{:T(128)}, f32[2,64,1024]{2,1,0:T(8,128)S(1)}, ...), condition=%wide.region_2.2_spmd, body=%wide.region_1.1_spmd.sunk | while | flops 134414336 | bytes 4194599 | solution.py:80
  134.9 10.5 collective-permute-done.5
  148.4 7.9 collective-permute-start.3
  161.4 44.5 %while.86 = (s32[]{:T(128)}, f32[2,64,1024]{2,1,0:T(8,128)S(1)}, s32[]{:T(128)}, s32[6]{0:T(128)S(1)}, s32[6]{0:T(128)S(1)}, /*index=5*/bf16[2,64,3072]{2,1,0:T(...) while((s32[]{:T(128)}, f32[2,64,1024]{2,1,0:T(8,128)S(1)}, ...), condition=%wide.region_2.2_spmd, body=%wide.region_1.1_spmd.sunk | while | flops 134414336 | bytes 4194599 | solution.py:80
  205.9 12.7 collective-permute-start.5
  234.1 59.0 %collective-permute-start.5 = (bf16[2,64,1024]{2,1,0:T(8,128)(2,1)S(1)}, bf16[2,64,1024]{2,1,0:T(8,128)(2,1)S(1)}, u32[]{:S(2)}, u32[]{:S(2)}) collective-permute-start(bf16[2,64,1024]{2,1,0:T(8,128)(2,1)S(1)} %convert_element_type.115), channel_id=1, source_target_pairs={{0,32},{32,64},{64,96},{96,128},{128,160},{160,192},{192,224},{1,3... | collective-permute-start | bytes 786440 | tf_op jit(solution)/shard_map/while/body/eval_jaxpr/ppermute | solution.py:26
  320.2 6.2 collective-permute-start.3
  329.9 45.3 %collective-permute-start.5 = (bf16[2,64,1024]{2,1,0:T(8,128)(2,1)S(1)}, bf16[2,64,1024]{2,1,0:T(8,128)(2,1)S(1)}, u32[]{:S(2)}, u32[]{:S(2)}) collective-permute-start(bf16[2,64,1024]{2,1,0:T(8,128)(2,1)S(1)} %convert_element_type.115), channel_id=1, source_target_pairs={{0,32},{32,64},{64,96},{96,128},{128,160},{160,192},{192,224},{1,3... | collective-permute-start | bytes 786440 | tf_op jit(solution)/shard_map/while/body/eval_jaxpr/ppermute | solution.py:26
  390.9 5.8 collective-permute-start.5
  412.1 49.3 %collective-permute-start.5 = (bf16[2,64,1024]{2,1,0:T(8,128)(2,1)S(1)}, bf16[2,64,1024]{2,1,0:T(8,128)(2,1)S(1)}, u32[]{:S(2)}, u32[]{:S(2)}) collective-permute-start(bf16[2,64,1024]{2,1,0:T(8,128)(2,1)S(1)} %convert_element_type.115), channel_id=1, source_target_pairs={{0,32},{32,64},{64,96},{96,128},{128,160},{160,192},{192,224},{1,3... | collective-permute-start | bytes 786440 | tf_op jit(solution)/shard_map/while/body/eval_jaxpr/ppermute | solution.py:26
  476.7 5.6 collective-permute-start.5
  485.7 786.5 %while.85 = (s32[]{:T(128)}, bf16[2,64,1024]{2,1,0:T(8,128)(2,1)S(1)}, bf16[2,128,1024]{2,1,0:T(8,128)(2,1)S(1)}, s32[]{:T(128)}, s32[]{:T(128)}, /*index=5*/bf1...) while((s32[]{:T(128)}, ...), condition=%wide.region_7.8_spmd, body=%wide.region_4.7_spmd.sunk | while | flops 136118288 | bytes 14943049 | solution.py:126
  486.8 6.1 collective-permute-start
  496.3 5.9 collective-permute-done.1
  504.2 51.8 %collective-permute-done.2 = bf16[2,64,1024]{2,1,0:T(8,128)(2,1)S(1)} collective-permute-done((bf16[2,64,1024]{2,1,0:T(8,128)(2,1)S(1)}, bf16[2,64,1024]{2,1,0:T(8,128)(2,1)S(1)}, u32[]{:S(2)}, u32[]{:S(2)}) %collective-permute-start.2) | collective-permute-done | bytes 262176 | tf_op jit(solution)/shard_map/while/body/eval_jaxpr/ppermute | solution.py:26
  570.3 6.8 collective-permute-done.2
  591.4 56.9 %collective-permute-done.2 = bf16[2,64,1024]{2,1,0:T(8,128)(2,1)S(1)} collective-permute-done((bf16[2,64,1024]{2,1,0:T(8,128)(2,1)S(1)}, bf16[2,64,1024]{2,1,0:T(8,128)(2,1)S(1)}, u32[]{:S(2)}, u32[]{:S(2)}) %collective-permute-start.2) | collective-permute-done | bytes 262176 | tf_op jit(solution)/shard_map/while/body/eval_jaxpr/ppermute | solution.py:26
  662.7 6.8 collective-permute-done.2
  683.8 50.0 %collective-permute-done.2 = bf16[2,64,1024]{2,1,0:T(8,128)(2,1)S(1)} collective-permute-done((bf16[2,64,1024]{2,1,0:T(8,128)(2,1)S(1)}, bf16[2,64,1024]{2,1,0:T(8,128)(2,1)S(1)}, u32[]{:S(2)}, u32[]{:S(2)}) %collective-permute-start.2) | collective-permute-done | bytes 262176 | tf_op jit(solution)/shard_map/while/body/eval_jaxpr/ppermute | solution.py:26
  748.1 313.6 %collective-permute-done.2 = bf16[2,64,1024]{2,1,0:T(8,128)(2,1)S(1)} collective-permute-done((bf16[2,64,1024]{2,1,0:T(8,128)(2,1)S(1)}, bf16[2,64,1024]{2,1,0:T(8,128)(2,1)S(1)}, u32[]{:S(2)}, u32[]{:S(2)}) %collective-permute-start.2) | collective-permute-done | bytes 262176 | tf_op jit(solution)/shard_map/while/body/eval_jaxpr/ppermute | solution.py:26
  1062.7 43.9 %while.87 = (s32[]{:T(128)}, f32[2,64,3072]{2,1,0:T(8,128)S(1)}, s32[]{:T(128)}, s32[6]{0:T(128)S(1)}, s32[6]{0:T(128)S(1)}, /*index=5*/bf16[2,64,1024]{2,1,0:T(...) while((s32[]{:T(128)}, f32[2,64,3072]{2,1,0:T(8,128)S(1)}, ...), condition=%wide.region_6.6_spmd, body=%wide.region_5.5_spmd.sunk | while | flops 134414336 | bytes 4194599 | solution.py:110
  1106.7 11.2 collective-permute-start
  1121.2 5.9 collective-permute-done.1
  1129.2 5.8 collective-permute-done.2
  1135.9 43.9 %while.87 = (s32[]{:T(128)}, f32[2,64,3072]{2,1,0:T(8,128)S(1)}, s32[]{:T(128)}, s32[6]{0:T(128)S(1)}, s32[6]{0:T(128)S(1)}, /*index=5*/bf16[2,64,1024]{2,1,0:T(...) while((s32[]{:T(128)}, f32[2,64,3072]{2,1,0:T(8,128)S(1)}, ...), condition=%wide.region_6.6_spmd, body=%wide.region_5.5_spmd.sunk | while | flops 134414336 | bytes 4194599 | solution.py:110
  1180.0 10.2 collective-permute-start
  1193.5 5.9 collective-permute-done.1
  1201.5 5.8 collective-permute-done.2
  1219.6 51.4 %collective-permute-start.2 = (bf16[2,64,1024]{2,1,0:T(8,128)(2,1)S(1)}, bf16[2,64,1024]{2,1,0:T(8,128)(2,1)S(1)}, u32[]{:S(2)}, u32[]{:S(2)}) collective-permute-start(bf16[2,64,1024]{2,1,0:T(8,128)(2,1)S(1)} %add_convert_fusion.6), channel_id=1, source_target_pairs={{32,0},{64,32},{96,64},{128,96},{160,128},{192,160},{224,192},{33,... | collective-permute-start | bytes 786440 | tf_op jit(solution)/shard_map/while/body/eval_jaxpr/ppermute | solution.py:26
  (346 shorter events, 319.9 us)
Async XLA Ops:
  2.6 13.8 %collective-permute-start.4 = (bf16[2,64,1024]{2,1,0:T(8,128)(2,1)S(1)}, bf16[2,64,1024]{2,1,0:T(8,128)(2,1)S(1)}, u32[]{:S(2)}, u32[]{:S(2)}) collective-permute-start(bf16[2,64,1024]{2,1,0:T(8,128)(2,1)S(1)} %get-tuple-element.737), channel_id=1, source_target_pairs={{0,1},{1,2},{2,3},{3,4},{4,5},{5,6},{6,7},{7,8},{8,9},{9,10},{10,1... | collective-permute-start | bytes 786440 | tf_op jit(solution)/shard_map/while/body/eval_jaxpr/ppermute | solution.py:17
  6.1 11.1 collective-permute-start.3
  17.4 57.2 %collective-permute-start.5 = (bf16[2,64,1024]{2,1,0:T(8,128)(2,1)S(1)}, bf16[2,64,1024]{2,1,0:T(8,128)(2,1)S(1)}, u32[]{:S(2)}, u32[]{:S(2)}) collective-permute-start(bf16[2,64,1024]{2,1,0:T(8,128)(2,1)S(1)} %convert_element_type.115), channel_id=1, source_target_pairs={{0,32},{32,64},{64,96},{96,128},{128,160},{160,192},{192,224},{1,3... | collective-permute-start | bytes 786440 | tf_op jit(solution)/shard_map/while/body/eval_jaxpr/ppermute | solution.py:26
  75.6 11.7 collective-permute-start.4
  77.6 10.7 collective-permute-start.3
  132.9 12.4 collective-permute-start.5
  146.5 13.0 %collective-permute-start.4 = (bf16[2,64,1024]{2,1,0:T(8,128)(2,1)S(1)}, bf16[2,64,1024]{2,1,0:T(8,128)(2,1)S(1)}, u32[]{:S(2)}, u32[]{:S(2)}) collective-permute-start(bf16[2,64,1024]{2,1,0:T(8,128)(2,1)S(1)} %get-tuple-element.737), channel_id=1, source_target_pairs={{0,1},{1,2},{2,3},{3,4},{4,5},{5,6},{6,7},{7,8},{8,9},{9,10},{10,1... | collective-permute-start | bytes 786440 | tf_op jit(solution)/shard_map/while/body/eval_jaxpr/ppermute | solution.py:17
  148.4 12.9 %collective-permute-start.3 = (bf16[2,64,1024]{2,1,0:T(8,128)(2,1)S(1)}, bf16[2,64,1024]{2,1,0:T(8,128)(2,1)S(1)}, u32[]{:S(2)}, u32[]{:S(2)}) collective-permute-start(bf16[2,64,1024]{2,1,0:T(8,128)(2,1)S(1)} %get-tuple-element.737), channel_id=1, source_target_pairs={{1,0},{2,1},{3,2},{4,3},{5,4},{6,5},{7,6},{8,7},{9,8},{10,9},{11,1... | collective-permute-start | bytes 786440 | tf_op jit(solution)/shard_map/while/body/eval_jaxpr/ppermute | solution.py:18
  205.9 16.0 %collective-permute-start.5 = (bf16[2,64,1024]{2,1,0:T(8,128)(2,1)S(1)}, bf16[2,64,1024]{2,1,0:T(8,128)(2,1)S(1)}, u32[]{:S(2)}, u32[]{:S(2)}) collective-permute-start(bf16[2,64,1024]{2,1,0:T(8,128)(2,1)S(1)} %convert_element_type.115), channel_id=1, source_target_pairs={{0,32},{32,64},{64,96},{96,128},{128,160},{160,192},{192,224},{1,3... | collective-permute-start | bytes 786440 | tf_op jit(solution)/shard_map/while/body/eval_jaxpr/ppermute | solution.py:26
  223.0 9.2 collective-permute-start.4
  234.1 62.3 %collective-permute-start.5 = (bf16[2,64,1024]{2,1,0:T(8,128)(2,1)S(1)}, bf16[2,64,1024]{2,1,0:T(8,128)(2,1)S(1)}, u32[]{:S(2)}, u32[]{:S(2)}) collective-permute-start(bf16[2,64,1024]{2,1,0:T(8,128)(2,1)S(1)} %convert_element_type.115), channel_id=1, source_target_pairs={{0,32},{32,64},{64,96},{96,128},{128,160},{160,192},{192,224},{1,3... | collective-permute-start | bytes 786440 | tf_op jit(solution)/shard_map/while/body/eval_jaxpr/ppermute | solution.py:26
  297.5 9.2 collective-permute-start.4
  318.3 10.0 collective-permute-start.4
  320.2 9.5 collective-permute-start.3
  329.9 48.6 %collective-permute-start.5 = (bf16[2,64,1024]{2,1,0:T(8,128)(2,1)S(1)}, bf16[2,64,1024]{2,1,0:T(8,128)(2,1)S(1)}, u32[]{:S(2)}, u32[]{:S(2)}) collective-permute-start(bf16[2,64,1024]{2,1,0:T(8,128)(2,1)S(1)} %convert_element_type.115), channel_id=1, source_target_pairs={{0,32},{32,64},{64,96},{96,128},{128,160},{160,192},{192,224},{1,3... | collective-permute-start | bytes 786440 | tf_op jit(solution)/shard_map/while/body/eval_jaxpr/ppermute | solution.py:26
  401.1 9.3 collective-permute-start.4
  412.1 52.6 %collective-permute-start.5 = (bf16[2,64,1024]{2,1,0:T(8,128)(2,1)S(1)}, bf16[2,64,1024]{2,1,0:T(8,128)(2,1)S(1)}, u32[]{:S(2)}, u32[]{:S(2)}) collective-permute-start(bf16[2,64,1024]{2,1,0:T(8,128)(2,1)S(1)} %convert_element_type.115), channel_id=1, source_target_pairs={{0,32},{32,64},{64,96},{96,128},{128,160},{160,192},{192,224},{1,3... | collective-permute-start | bytes 786440 | tf_op jit(solution)/shard_map/while/body/eval_jaxpr/ppermute | solution.py:26
  465.8 9.2 collective-permute-start.4
  486.8 9.4 collective-permute-start
  493.0 9.2 collective-permute-start.1
  502.3 53.7 %collective-permute-start.2 = (bf16[2,64,1024]{2,1,0:T(8,128)(2,1)S(1)}, bf16[2,64,1024]{2,1,0:T(8,128)(2,1)S(1)}, u32[]{:S(2)}, u32[]{:S(2)}) collective-permute-start(bf16[2,64,1024]{2,1,0:T(8,128)(2,1)S(1)} %add_convert_fusion.6), channel_id=1, source_target_pairs={{32,0},{64,32},{96,64},{128,96},{160,128},{192,160},{224,192},{33,... | collective-permute-start | bytes 786440 | tf_op jit(solution)/shard_map/while/body/eval_jaxpr/ppermute | solution.py:26
  559.1 9.2 collective-permute-start.1
  580.2 9.2 collective-permute-start.1
  589.5 58.8 %collective-permute-start.2 = (bf16[2,64,1024]{2,1,0:T(8,128)(2,1)S(1)}, bf16[2,64,1024]{2,1,0:T(8,128)(2,1)S(1)}, u32[]{:S(2)}, u32[]{:S(2)}) collective-permute-start(bf16[2,64,1024]{2,1,0:T(8,128)(2,1)S(1)} %add_convert_fusion.6), channel_id=1, source_target_pairs={{32,0},{64,32},{96,64},{128,96},{160,128},{192,160},{224,192},{33,... | collective-permute-start | bytes 786440 | tf_op jit(solution)/shard_map/while/body/eval_jaxpr/ppermute | solution.py:26
  681.8 52.0 %collective-permute-start.2 = (bf16[2,64,1024]{2,1,0:T(8,128)(2,1)S(1)}, bf16[2,64,1024]{2,1,0:T(8,128)(2,1)S(1)}, u32[]{:S(2)}, u32[]{:S(2)}) collective-permute-start(bf16[2,64,1024]{2,1,0:T(8,128)(2,1)S(1)} %add_convert_fusion.6), channel_id=1, source_target_pairs={{32,0},{64,32},{96,64},{128,96},{160,128},{192,160},{224,192},{33,... | collective-permute-start | bytes 786440 | tf_op jit(solution)/shard_map/while/body/eval_jaxpr/ppermute | solution.py:26
  736.9 9.2 collective-permute-start.1
  746.2 315.5 %collective-permute-start.2 = (bf16[2,64,1024]{2,1,0:T(8,128)(2,1)S(1)}, bf16[2,64,1024]{2,1,0:T(8,128)(2,1)S(1)}, u32[]{:S(2)}, u32[]{:S(2)}) collective-permute-start(bf16[2,64,1024]{2,1,0:T(8,128)(2,1)S(1)} %add_convert_fusion.6), channel_id=1, source_target_pairs={{32,0},{64,32},{96,64},{128,96},{160,128},{192,160},{224,192},{33,... | collective-permute-start | bytes 786440 | tf_op jit(solution)/shard_map/while/body/eval_jaxpr/ppermute | solution.py:26
  1106.7 14.5 %collective-permute-start = (bf16[2,64,1024]{2,1,0:T(8,128)(2,1)S(1)}, bf16[2,64,1024]{2,1,0:T(8,128)(2,1)S(1)}, u32[]{:S(2)}, u32[]{:S(2)}) collective-permute-start(bf16[2,64,1024]{2,1,0:T(8,128)(2,1)S(1)} %get-tuple-element.752), channel_id=1, source_target_pairs={{1,0},{2,1},{3,2},{4,3},{5,4},{6,5},{7,6},{8,7},{9,8},{10,9},{11,1... | collective-permute-start | bytes 786440 | tf_op jit(solution)/shard_map/while/body/eval_jaxpr/ppermute | solution.py:26
  1180.0 13.5 %collective-permute-start = (bf16[2,64,1024]{2,1,0:T(8,128)(2,1)S(1)}, bf16[2,64,1024]{2,1,0:T(8,128)(2,1)S(1)}, u32[]{:S(2)}, u32[]{:S(2)}) collective-permute-start(bf16[2,64,1024]{2,1,0:T(8,128)(2,1)S(1)} %get-tuple-element.752), channel_id=1, source_target_pairs={{1,0},{2,1},{3,2},{4,3},{5,4},{6,5},{7,6},{8,7},{9,8},{10,9},{11,1... | collective-permute-start | bytes 786440 | tf_op jit(solution)/shard_map/while/body/eval_jaxpr/ppermute | solution.py:26
  1190.2 9.2 collective-permute-start.1
  1210.3 9.2 collective-permute-start.1
  1219.6 52.5 %collective-permute-start.2 = (bf16[2,64,1024]{2,1,0:T(8,128)(2,1)S(1)}, bf16[2,64,1024]{2,1,0:T(8,128)(2,1)S(1)}, u32[]{:S(2)}, u32[]{:S(2)}) collective-permute-start(bf16[2,64,1024]{2,1,0:T(8,128)(2,1)S(1)} %add_convert_fusion.6), channel_id=1, source_target_pairs={{32,0},{64,32},{96,64},{128,96},{160,128},{192,160},{224,192},{33,... | collective-permute-start | bytes 786440 | tf_op jit(solution)/shard_map/while/body/eval_jaxpr/ppermute | solution.py:26
  (24 other events, 180.4 us)
where the time goes:
time: 1280 us; the launch traced here: 1270 us
  waiting for transfers between devices  671 us (52%)
  starting transfers between devices  394 us (31%)
  loops' own time  97.6 us (8%)
  matrix products  52.4 us (4%)
  local copies, waits for them, and re-layouts  39.4 us (3%)
  other arithmetic  18.1 us (1%)
    ppermute x36, waiting for transfers between devices, from_behind(): return lax.ppermute(block, axis, route)  642 us
    ppermute x36, starting transfers between devices, from_behind(): return lax.ppermute(block, axis, route)  322 us
    ppermute x9, starting transfers between devices, padded(): after = lax.ppermute(initial, axis, down)  48.1 us
    another operation x9, loops' own time, down_step(): lax.fori_loop(0, jnp.where(active, live_count, 0), down_add_tile, jnp.zer...  42.3 us
    another operation x9, loops' own time, up_step(): lax.fori_loop(0, jnp.where(active, live_count, 0), up_add_tile, jnp.zeros...  42.3 us
    dot_general x20, matrix products, complex_apply(): lax.dot_general(flattened, matrix[1], numbers, preferred_element_type=jnp...  26.2 us
    dot_general x20, matrix products, complex_apply(): lax.dot_general(flattened, matrix[0], numbers, preferred_element_type=jnp...  26.2 us
  transfers between devices with their start and end apart: 54, of which 54 were waited for; matrix products, arithmetic and copies ran while one was open for 0% of the time, Pallas kernels for 0%

commit v1 on v0

v1 whole, which is shorter than its diff:
```python
import functools

import jax
import jax.numpy as jnp
from jax import lax
from jax.experimental import pallas as pl
from jax.experimental.pallas import tpu as pltpu
from jax.sharding import PartitionSpec as P

WAVES = 2
PITCH = 3
ORDER = (0, 1, -1)
AXES = ("layer", "blk")
F32, BF16 = jnp.float32, jnp.bfloat16
META = 4


def schedule(layers):
    top = layers - 1
    steps = []
    for step in range(2 * top + 1 + PITCH * (WAVES - 1)):
        waves = []
        for b in range(WAVES):
            t = step - PITCH * b
            if 0 <= t < top:
                waves.append((b, t, 1, t))
            elif top <= t < 2 * top:
                waves.append((b, 2 * top - t, 3 if t == top else 2, 2 * top - t - 1))
            elif t == 2 * top:
                waves.append((b, 0, 4, None))
        steps.append(waves)
    return steps


def route(hops, shift, layers, ranges):
    to = {i: i for i in range(layers * ranges)}
    for k in hops:
        for g in range(max(0, -shift), ranges - max(0, shift)):
            a, b = k * ranges + g, (k + 1) * ranges + g + shift
            to[a], to[b] = b, a
    return sorted(to.items())


def stacked(real, imag):
    return jnp.concatenate(
        [jnp.concatenate([real, imag], axis=0), jnp.concatenate([-imag, real], axis=0)], axis=1
    )


def step_kernel(waves, has_halo, meta, tiles, here, left, right, below, down_in, up_in, *rest):
    downs = [w for w in waves if w[2] == 1]
    ups = [w for w in waves if w[2] != 1]
    if has_halo:
        halo_l, halo_r, *rest = rest
    n_send = 3 if ups else 1
    sends, (down_all, up_all, lhs, acc) = rest[:n_send], rest[n_send:]
    shots = here.shape[1]
    tile = tiles.shape[2]
    layer, count = meta[0], meta[1]
    slots = (meta.shape[0] - META) // 2
    mode, wave = jnp.int32(0), jnp.int32(0)
    for b, at, code, _ in waves:
        mode = jnp.where(layer == at, code, mode)
        wave = jnp.where(layer == at, b, wave)
    mine = pl.ds(pl.multiple_of(wave * shots, shots), shots)

    def product(slot, source, contract):
        numbers = (((1,), (contract,)), ((), ()))
        x = lhs[source]
        return lax.dot_general(x[:, :tile], tiles[slot, 0], numbers, preferred_element_type=F32) + (
            lax.dot_general(x[:, tile:], tiles[slot, 1], numbers, preferred_element_type=F32)
        )

    def fill(index, ref, rows=slice(None)):
        for j in range(2):
            piece = slice(j * tile, (j + 1) * tile)
            lhs[index + j] = stacked(ref[0, rows, piece], ref[1, rows, piece])

    def next_down():
        fill(0, left)
        fill(2, here)
        fill(4, right)
        down_all[0, mine, :] = here[0]
        down_all[1, mine, :] = here[1]

    def first():
        fill(0, halo_l)
        fill(2, down_all, mine)
        fill(4, halo_r)

    def down():
        for j in range(2):
            acc[j] = jnp.zeros(acc.shape[1:], F32)

        def one(slot, carry):
            acc[meta[META + slot]] += product(slot, meta[META + slots + slot], 1)
            return carry

        lax.fori_loop(0, count, one, 0)
        for j in range(2):
            piece = slice(j * tile, (j + 1) * tile)
            for part in range(2):
                summed = acc[j, part * shots : (part + 1) * shots].astype(BF16).astype(F32)
                value = (summed + below[part, mine, piece].astype(F32)).astype(BF16)
                for send in sends:
                    send[part, :, piece] = value

    def next_up():
        zero = jnp.zeros((shots, tile), F32)
        for j in range(2):
            piece = slice(j * tile, (j + 1) * tile)
            halves = []
            for part in range(2):
                sums = here[part, :, piece].astype(F32)
                sums += jnp.where(meta[3] > 0, left[part, :, piece].astype(F32), zero)
                sums += jnp.where(meta[2] > 0, right[part, :, piece].astype(F32), zero)
                sums = sums.astype(BF16).astype(F32)
                value = (down_all[part, mine, piece].astype(F32) + sums).astype(BF16)
                up_all[part, mine, piece] = value
                halves.append(value)
            lhs[j] = stacked(*halves)

    def turn():
        for part in range(2):
            value = here[part]
            down_all[part, mine, :] = value
            up_all[part, mine, :] = value
        fill(0, here)

    def up():
        for j in range(6):
            acc[j] = jnp.zeros(acc.shape[1:], F32)

        def one(slot, carry):
            acc[meta[META + slots + slot]] += product(slot, meta[META + slot], 0)
            return carry

        lax.fori_loop(0, count, one, 0)
        for shift, send in zip((0, 1, -1), sends):
            for j in range(2):
                for part in range(2):
                    send[part, :, j * tile : (j + 1) * tile] = acc[
                        2 - 2 * shift + j, part * shots : (part + 1) * shots
                    ].astype(BF16)

    if has_halo:
        pl.when((mode == 1) & (layer == 0))(first)
    if any(at > 0 for _, at, _, _ in downs):
        pl.when((mode == 1) & (layer > 0))(next_down)
    if any(code == 3 for _, _, code, _ in ups):
        pl.when(mode == 3)(turn)
    if any(code in (2, 4) for _, _, code, _ in ups):
        pl.when((mode == 2) | (mode == 4))(next_up)
    if downs:
        pl.when(mode == 1)(down)
    if any(code in (2, 3) for _, _, code, _ in ups):
        pl.when((mode == 2) | (mode == 3))(up)


VMEM = pl.BlockSpec(memory_space=pltpu.VMEM)
SMEM = pl.BlockSpec(memory_space=pltpu.SMEM)


def run_step(waves, meta, tiles, here, left, right, below, down_all, up_all, halo):
    shots = here.shape[1]
    tile = tiles.shape[2]
    n_send = 3 if any(code != 1 for _, _, code, _ in waves) else 1
    return pl.pallas_call(
        functools.partial(step_kernel, waves, bool(halo)),
        out_shape=[pltpu.VMEM(here.shape, BF16)] * n_send + [pltpu.VMEM(down_all.shape, BF16)] * 2,
        in_specs=[SMEM] + [VMEM] * (7 + len(halo)),
        out_specs=[VMEM] * (n_send + 2),
        input_output_aliases={6: n_send, 7: n_send + 1},
        scratch_shapes=[
            pltpu.VMEM((6, 2 * shots, 2 * tile), BF16),
            pltpu.VMEM((6, 2 * shots, tile), F32),
        ],
        compiler_params=pltpu.CompilerParams(vmem_limit_bytes=24 << 20),
        name="step",
    )(meta, *map(resident, (tiles, here, left, right, below, down_all, up_all, *halo)))


def resident(x):
    return pltpu.with_memory_space_constraint(x, pltpu.VMEM)


def on_device(source, tile_data, tile_rows, tile_cols, tile_count):
    layers, ranges = lax.axis_size("layer"), lax.axis_size("blk")
    layer, rng = lax.axis_index("layer"), lax.axis_index("blk")
    own = source.shape[3] // tile_data.shape[3]
    first = rng * own
    meta = jnp.concatenate(
        [
            jnp.stack([layer, tile_count[0, 0], (rng > 0).astype(jnp.int32), (rng < ranges - 1).astype(jnp.int32)]),
            tile_rows[0] - first,
            tile_cols[0] - first + own,
        ]
    )
    sources = source[0]
    shots = source.shape[2] // WAVES

    def part(b):
        return lax.slice_in_dim(sources, b * shots, (b + 1) * shots, axis=1)

    def around(x, shift):
        return lax.ppermute(x, "blk", [(g, (g + shift) % ranges) for g in range(ranges)])

    halos = [(around(part(b), 1), around(part(b), -1)) for b in range(WAVES)]
    below = lax.ppermute(
        sources,
        AXES,
        [(((l + 1) % layers) * ranges + g, l * ranges + g) for l in range(layers) for g in range(ranges)],
    )
    tiles = tile_data[0]
    down_all, up_all = sources, jnp.zeros_like(sources)
    here = left = right = part(0)
    for waves in schedule(layers):
        halo = [h for b, at, code, _ in waves if code == 1 and at == 0 for h in halos[b]]
        *sends, down_all, up_all = run_step(
            waves, meta, tiles, here, left, right, below, down_all, up_all, halo
        )
        sends = dict(zip((0, 1, -1), sends * (3 // len(sends))))
        hops = sorted({hop for *_, hop in waves if hop is not None})
        if hops:
            got = {s: lax.ppermute(sends[s], AXES, route(hops, s, layers, ranges)) for s in ORDER}
            here, left, right = got[0], got[1], got[-1]
    return (down_all[None], up_all[None])


def solution(mesh):
    in_specs = (
        P("layer", None, None, "blk"),
        P("layer", "blk", None, None, None),
        P("layer", "blk"),
        P("layer", "blk"),
        P("layer", "blk"),
    )
    out_specs = (P("layer", None, None, "blk"), P("layer", None, None, "blk"))
    return jax.shard_map(
        on_device, mesh=mesh, in_specs=in_specs, out_specs=out_specs, check_vma=False
    )
```

time: 1280 us -> 320 us (0.25)
  waiting for transfers between devices: 671 us -> 56.9 us
  starting transfers between devices: 394 us -> 232 us
  loops' own time: 97.6 us -> 0 us
  matrix products: 52.4 us -> 0 us
  local copies, waits for them, and re-layouts: 39.4 us -> 5.58 us
  Pallas kernels: 0 us -> 18.7 us
  other arithmetic: 18.1 us -> 0.68 us
    ppermute x54 -> x56, waiting for transfers between devices: 671 us -> 56.9 us  [the longest x51 51 us: on_device(): lax.ppermute(sends[s], AXES, route(hops, s, layers, ranges))]
    ppermute x54 -> x56, starting transfers between devices: 394 us -> 232 us  [the longest x51 223 us: on_device(): lax.ppermute(sends[s], AXES, route(hops, s, layers, ranges))]
    another operation x20 -> x0, loops' own time: 97.6 us -> none  [the longest x9 42.3 us: down_step(): lax.fori_loop(0, jnp.where(active, live_count, 0), down_add_tile, jnp.zer...]
    dot_general x40 -> x0, matrix products: 52.4 us -> none  [the longest x20 26.2 us: complex_apply(): lax.dot_general(flattened, matrix[1], numbers, preferred_element_type=jnp...]
    dynamic_slice x60 -> x0, local copies, waits for them, and re-layouts: 28.8 us -> none  [the longest x10 6.66 us: up_add_tile(): row_start[slot_index]]
    pallas_call x0 -> x18, Pallas kernels: none -> 18.7 us  [run_step(): pl.pallas_call(functools.partial(step_kernel, waves, bool(halo)), out_sha...]
  transfers between devices with their start and end apart: 54 -> 56, of which waited for: 54 -> 19; matrix products, arithmetic and copies ran while one was open for 0% -> 0% of each run, Pallas kernels for 0% -> 0%
where the time goes in v1:
time: 320 us; the launch traced here: 316 us
  starting transfers between devices  232 us (72%)
  waiting for transfers between devices  56.9 us (18%)
  Pallas kernels  18.7 us (6%)
  local copies, waits for them, and re-layouts  5.58 us (2%)
    ppermute x51, starting transfers between devices, on_device(): lax.ppermute(sends[s], AXES, route(hops, s, layers, ranges))  223 us
    ppermute x51, waiting for transfers between devices, on_device(): lax.ppermute(sends[s], AXES, route(hops, s, layers, ranges))  51 us
    pallas_call x18, Pallas kernels, run_step(): pl.pallas_call(functools.partial(step_kernel, waves, bool(halo)), out_sha...  18.7 us
    ppermute x4, starting transfers between devices, around(): lax.ppermute(x, 'blk', [(g, (g + shift) % ranges) for g in range(ranges)])  7.95 us
  transfers between devices with their start and end apart: 56, of which 19 were waited for; matrix products, arithmetic and copies ran while one was open for 0% of the time, Pallas kernels for 0%

profile of v1, /device:TPU:7, one launch (start us, length us, event | category | flops | bytes accessed | tf_op | source)
XLA Modules:
  0.0 315.8 jit_solution(17840630283278657670)
XLA Ops:
  2.4 5.9 %collective-permute-start.2 = (bf16[2,64,1024]{2,1,0:T(8,128)(2,1)S(1)}, bf16[2,64,1024]{2,1,0:T(8,128)(2,1)S(1)}, u32[]{:S(2)}, u32[]{:S(2)}) collective-permute-start(bf16[2,64,1024]{2,1,0:T(8,128)(2,1)S(1)} %get-tuple-element.149.here.left.right), channel_id=1, source_target_pairs={{0,31},{1,0},{2,1},{3,2},{4,3},{5,4},{6,5},{7,6},{8,7},{9,8},{10,9... | collective-permute-start | bytes 786440 | tf_op jit(solution)/shard_map/ppermute | solution.py:206
  11.6 4.0 %collective-permute-done.1.rest_0_ = bf16[2,64,1024]{2,1,0:T(8,128)(2,1)S(1)} collective-permute-done((bf16[2,64,1024]{2,1,0:T(8,128)(2,1)S(1)}, bf16[2,64,1024]{2,1,0:T(8,128)(2,1)S(1)}, u32[]{:S(2)}, u32[]{:S(2)}) %collective-permute-start.1) | collective-permute-done | bytes 262176 | tf_op jit(solution)/shard_map/ppermute | solution.py:206
  15.7 2.8 copy-done
  19.1 5.9 %collective-permute-start.5 = (bf16[2,64,1024]{2,1,0:T(8,128)(2,1)S(1)}, bf16[2,64,1024]{2,1,0:T(8,128)(2,1)S(1)}, u32[]{:S(2)}, u32[]{:S(2)}) collective-permute-start(bf16[2,64,1024]{2,1,0:T(8,128)(2,1)S(1)} %get-tuple-element.75), channel_id=1, source_target_pairs={{0,0},{1,32},{2,33},{3,34},{4,35},{5,36},{6,37},{7,38},{8,39},{9,4... | collective-permute-start | bytes 786440 | tf_op jit(solution)/shard_map/ppermute | solution.py:225
  24.9 4.0 %collective-permute-start.4 = (bf16[2,64,1024]{2,1,0:T(8,128)(2,1)S(1)}, bf16[2,64,1024]{2,1,0:T(8,128)(2,1)S(1)}, u32[]{:S(2)}, u32[]{:S(2)}) collective-permute-start(bf16[2,64,1024]{2,1,0:T(8,128)(2,1)S(1)} %get-tuple-element.75), channel_id=1, source_target_pairs={{0,33},{1,34},{2,35},{3,36},{4,37},{5,38},{6,39},{7,40},{8,41},{9,... | collective-permute-start | bytes 786440 | tf_op jit(solution)/shard_map/ppermute | solution.py:225
  30.9 6.0 %collective-permute-done.4.left = bf16[2,64,1024]{2,1,0:T(8,128)(2,1)S(1)} collective-permute-done((bf16[2,64,1024]{2,1,0:T(8,128)(2,1)S(1)}, bf16[2,64,1024]{2,1,0:T(8,128)(2,1)S(1)}, u32[]{:S(2)}, u32[]{:S(2)}) %collective-permute-start.4) | collective-permute-done | bytes 262176 | tf_op jit(solution)/shard_map/ppermute | solution.py:225
  37.0 2.7 step.19
  43.5 5.0 %collective-permute-start.6 = (bf16[2,64,1024]{2,1,0:T(8,128)(2,1)S(1)}, bf16[2,64,1024]{2,1,0:T(8,128)(2,1)S(1)}, u32[]{:S(2)}, u32[]{:S(2)}) collective-permute-start(bf16[2,64,1024]{2,1,0:T(8,128)(2,1)S(1)} %get-tuple-element.78), channel_id=1, source_target_pairs={{0,0},{1,1},{2,2},{3,3},{4,4},{5,5},{6,6},{7,7},{8,8},{9,9},{10,10... | collective-permute-start | bytes 786440 | tf_op jit(solution)/shard_map/ppermute | solution.py:225
  48.5 2.0 collective-permute-start.13
  50.5 2.2 collective-permute-done.8.right
  53.1 2.7 collective-permute-done.6.here
  61.0 3.8 %collective-permute-start.15 = (bf16[2,64,1024]{2,1,0:T(8,128)(2,1)S(1)}, bf16[2,64,1024]{2,1,0:T(8,128)(2,1)S(1)}, u32[]{:S(2)}, u32[]{:S(2)}) collective-permute-start(bf16[2,64,1024]{2,1,0:T(8,128)(2,1)S(1)} %get-tuple-element.84), channel_id=1, source_target_pairs={{0,33},{1,34},{2,35},{3,36},{4,37},{5,38},{6,39},{7,40},{8,41},{9,... | collective-permute-start | bytes 786440 | tf_op jit(solution)/shard_map/ppermute | solution.py:225
  67.3 3.5 %collective-permute-done.15.left = bf16[2,64,1024]{2,1,0:T(8,128)(2,1)S(1)} collective-permute-done((bf16[2,64,1024]{2,1,0:T(8,128)(2,1)S(1)}, bf16[2,64,1024]{2,1,0:T(8,128)(2,1)S(1)}, u32[]{:S(2)}, u32[]{:S(2)}) %collective-permute-start.15) | collective-permute-done | bytes 262176 | tf_op jit(solution)/shard_map/ppermute | solution.py:225
  70.8 2.7 step.22
  73.5 5.3 %collective-permute-start.19 = (bf16[2,64,1024]{2,1,0:T(8,128)(2,1)S(1)}, bf16[2,64,1024]{2,1,0:T(8,128)(2,1)S(1)}, u32[]{:S(2)}, u32[]{:S(2)}) collective-permute-start(bf16[2,64,1024]{2,1,0:T(8,128)(2,1)S(1)} %get-tuple-element.87), channel_id=1, source_target_pairs={{0,0},{1,1},{2,2},{3,3},{4,4},{5,5},{6,6},{7,7},{8,8},{9,9},{10,10... | collective-permute-start | bytes 786440 | tf_op jit(solution)/shard_map/ppermute | solution.py:225
  80.7 2.4 collective-permute-start.17
  83.2 4.4 %collective-permute-done.19.right = bf16[2,64,1024]{2,1,0:T(8,128)(2,1)S(1)} collective-permute-done((bf16[2,64,1024]{2,1,0:T(8,128)(2,1)S(1)}, bf16[2,64,1024]{2,1,0:T(8,128)(2,1)S(1)}, u32[]{:S(2)}, u32[]{:S(2)}) %collective-permute-start.19) | collective-permute-done | bytes 262176 | tf_op jit(solution)/shard_map/ppermute | solution.py:225
  88.7 2.7 collective-permute-done.17.here
  110.8 120.6 %collective-permute-start.41 = (bf16[2,64,1024]{2,1,0:T(8,128)(2,1)S(1)}, bf16[2,64,1024]{2,1,0:T(8,128)(2,1)S(1)}, u32[]{:S(2)}, u32[]{:S(2)}) collective-permute-start(bf16[2,64,1024]{2,1,0:T(8,128)(2,1)S(1)} %get-tuple-element.121), channel_id=1, source_target_pairs={{0,0},{1,1},{2,2},{3,3},{4,4},{5,5},{6,6},{7,7},{8,8},{9,9},{10,10... | collective-permute-start | bytes 786440 | tf_op jit(solution)/shard_map/ppermute | solution.py:225
  233.4 3.1 collective-permute-start.43
  236.4 3.6 %collective-permute-done.42.left = bf16[2,64,1024]{2,1,0:T(8,128)(2,1)S(1)} collective-permute-done((bf16[2,64,1024]{2,1,0:T(8,128)(2,1)S(1)}, bf16[2,64,1024]{2,1,0:T(8,128)(2,1)S(1)}, u32[]{:S(2)}, u32[]{:S(2)}) %collective-permute-start.42) | collective-permute-done | bytes 262176 | tf_op jit(solution)/shard_map/ppermute | solution.py:225
  240.0 4.0 %collective-permute-done.43.right = bf16[2,64,1024]{2,1,0:T(8,128)(2,1)S(1)} collective-permute-done((bf16[2,64,1024]{2,1,0:T(8,128)(2,1)S(1)}, bf16[2,64,1024]{2,1,0:T(8,128)(2,1)S(1)}, u32[]{:S(2)}, u32[]{:S(2)}) %collective-permute-start.43) | collective-permute-done | bytes 262176 | tf_op jit(solution)/shard_map/ppermute | solution.py:225
  244.1 2.2 step.31
  248.2 4.4 %collective-permute-start.45 = (bf16[2,64,1024]{2,1,0:T(8,128)(2,1)S(1)}, bf16[2,64,1024]{2,1,0:T(8,128)(2,1)S(1)}, u32[]{:S(2)}, u32[]{:S(2)}) collective-permute-start(bf16[2,64,1024]{2,1,0:T(8,128)(2,1)S(1)} %get-tuple-element.127), channel_id=1, source_target_pairs={{0,33},{1,34},{2,35},{3,36},{4,37},{5,38},{6,39},{7,40},{8,41},{9,... | collective-permute-start | bytes 786440 | tf_op jit(solution)/shard_map/ppermute | solution.py:225
  254.6 4.8 %collective-permute-done.45.left = bf16[2,64,1024]{2,1,0:T(8,128)(2,1)S(1)} collective-permute-done((bf16[2,64,1024]{2,1,0:T(8,128)(2,1)S(1)}, bf16[2,64,1024]{2,1,0:T(8,128)(2,1)S(1)}, u32[]{:S(2)}, u32[]{:S(2)}) %collective-permute-start.45) | collective-permute-done | bytes 262176 | tf_op jit(solution)/shard_map/ppermute | solution.py:225
  263.8 19.8 %collective-permute-start.50 = (bf16[2,64,1024]{2,1,0:T(8,128)(2,1)S(1)}, bf16[2,64,1024]{2,1,0:T(8,128)(2,1)S(1)}, u32[]{:S(2)}, u32[]{:S(2)}) collective-permute-start(bf16[2,64,1024]{2,1,0:T(8,128)(2,1)S(1)} %get-tuple-element.136), channel_id=1, source_target_pairs={{0,0},{1,1},{2,2},{3,3},{4,4},{5,5},{6,6},{7,7},{8,8},{9,9},{10,10... | collective-permute-start | bytes 786440 | tf_op jit(solution)/shard_map/ppermute | solution.py:225
  285.5 3.1 collective-permute-start.52
  288.6 3.6 %collective-permute-done.51.left = bf16[2,64,1024]{2,1,0:T(8,128)(2,1)S(1)} collective-permute-done((bf16[2,64,1024]{2,1,0:T(8,128)(2,1)S(1)}, bf16[2,64,1024]{2,1,0:T(8,128)(2,1)S(1)}, u32[]{:S(2)}, u32[]{:S(2)}) %collective-permute-start.51) | collective-permute-done | bytes 262176 | tf_op jit(solution)/shard_map/ppermute | solution.py:225
  292.2 4.0 %collective-permute-done.52.right = bf16[2,64,1024]{2,1,0:T(8,128)(2,1)S(1)} collective-permute-done((bf16[2,64,1024]{2,1,0:T(8,128)(2,1)S(1)}, bf16[2,64,1024]{2,1,0:T(8,128)(2,1)S(1)}, u32[]{:S(2)}, u32[]{:S(2)}) %collective-permute-start.52) | collective-permute-done | bytes 262176 | tf_op jit(solution)/shard_map/ppermute | solution.py:225
  296.2 2.2 step.34
  300.4 4.4 %collective-permute-start.54 = (bf16[2,64,1024]{2,1,0:T(8,128)(2,1)S(1)}, bf16[2,64,1024]{2,1,0:T(8,128)(2,1)S(1)}, u32[]{:S(2)}, u32[]{:S(2)}) collective-permute-start(bf16[2,64,1024]{2,1,0:T(8,128)(2,1)S(1)} %get-tuple-element.142), channel_id=1, source_target_pairs={{0,33},{1,34},{2,35},{3,36},{4,37},{5,38},{6,39},{7,40},{8,41},{9,... | collective-permute-start | bytes 786440 | tf_op jit(solution)/shard_map/ppermute | solution.py:225
  306.7 4.8 %collective-permute-done.54.left = bf16[2,64,1024]{2,1,0:T(8,128)(2,1)S(1)} collective-permute-done((bf16[2,64,1024]{2,1,0:T(8,128)(2,1)S(1)}, bf16[2,64,1024]{2,1,0:T(8,128)(2,1)S(1)}, u32[]{:S(2)}, u32[]{:S(2)}) %collective-permute-start.54) | collective-permute-done | bytes 262176 | tf_op jit(solution)/shard_map/ppermute | solution.py:225
  (107 shorter events, 61.0 us)
Async XLA Ops:
  1.7 14.0 %collective-permute-start = (bf16[2,128,1024]{2,1,0:T(8,128)(2,1)S(1)}, bf16[2,128,1024]{2,1,0:T(8,128)(2,1)S(1)}, u32[]{:S(2)}, u32[]{:S(2)}) collective-permute-start(bf16[2,128,1024]{2,1,0:T(8,128)(2,1)S(1)} %bitcast.13), channel_id=1, source_target_pairs={{32,0},{33,1},{34,2},{35,3},{36,4},{37,5},{38,6},{39,7},{40,8},{41... | collective-permute-start | bytes 1572872 | tf_op jit(solution)/shard_map/ppermute | solution.py:209
  2.4 9.2 %collective-permute-start.2 = (bf16[2,64,1024]{2,1,0:T(8,128)(2,1)S(1)}, bf16[2,64,1024]{2,1,0:T(8,128)(2,1)S(1)}, u32[]{:S(2)}, u32[]{:S(2)}) collective-permute-start(bf16[2,64,1024]{2,1,0:T(8,128)(2,1)S(1)} %get-tuple-element.149.here.left.right), channel_id=1, source_target_pairs={{0,31},{1,0},{2,1},{3,2},{4,3},{5,4},{6,5},{7,6},{8,7},{9,8},{10,9... | collective-permute-start | bytes 786440 | tf_op jit(solution)/shard_map/ppermute | solution.py:206
  8.3 7.3 %collective-permute-start.1 = (bf16[2,64,1024]{2,1,0:T(8,128)(2,1)S(1)}, bf16[2,64,1024]{2,1,0:T(8,128)(2,1)S(1)}, u32[]{:S(2)}, u32[]{:S(2)}) collective-permute-start(bf16[2,64,1024]{2,1,0:T(8,128)(2,1)S(1)} %get-tuple-element.149.here.left.right), channel_id=1, source_target_pairs={{0,1},{1,2},{2,3},{3,4},{4,5},{5,6},{6,7},{7,8},{8,9},{9,10},{10,1... | collective-permute-start | bytes 786440 | tf_op jit(solution)/shard_map/ppermute | solution.py:206
  19.1 11.9 %collective-permute-start.5 = (bf16[2,64,1024]{2,1,0:T(8,128)(2,1)S(1)}, bf16[2,64,1024]{2,1,0:T(8,128)(2,1)S(1)}, u32[]{:S(2)}, u32[]{:S(2)}) collective-permute-start(bf16[2,64,1024]{2,1,0:T(8,128)(2,1)S(1)} %get-tuple-element.75), channel_id=1, source_target_pairs={{0,0},{1,32},{2,33},{3,34},{4,35},{5,36},{6,37},{7,38},{8,39},{9,4... | collective-permute-start | bytes 786440 | tf_op jit(solution)/shard_map/ppermute | solution.py:225
  24.9 12.0 %collective-permute-start.4 = (bf16[2,64,1024]{2,1,0:T(8,128)(2,1)S(1)}, bf16[2,64,1024]{2,1,0:T(8,128)(2,1)S(1)}, u32[]{:S(2)}, u32[]{:S(2)}) collective-permute-start(bf16[2,64,1024]{2,1,0:T(8,128)(2,1)S(1)} %get-tuple-element.75), channel_id=1, source_target_pairs={{0,33},{1,34},{2,35},{3,36},{4,37},{5,38},{6,39},{7,40},{8,41},{9,... | collective-permute-start | bytes 786440 | tf_op jit(solution)/shard_map/ppermute | solution.py:225
  29.0 8.0 %collective-permute-start.3 = (bf16[2,64,1024]{2,1,0:T(8,128)(2,1)S(1)}, bf16[2,64,1024]{2,1,0:T(8,128)(2,1)S(1)}, u32[]{:S(2)}, u32[]{:S(2)}) collective-permute-start(bf16[2,64,1024]{2,1,0:T(8,128)(2,1)S(1)} %get-tuple-element.75), channel_id=1, source_target_pairs={{0,32},{1,33},{2,34},{3,35},{4,36},{5,37},{6,38},{7,39},{8,40},{9,... | collective-permute-start | bytes 786440 | tf_op jit(solution)/shard_map/ppermute | solution.py:225
  39.7 13.1 %collective-permute-start.8 = (bf16[2,64,1024]{2,1,0:T(8,128)(2,1)S(1)}, bf16[2,64,1024]{2,1,0:T(8,128)(2,1)S(1)}, u32[]{:S(2)}, u32[]{:S(2)}) collective-permute-start(bf16[2,64,1024]{2,1,0:T(8,128)(2,1)S(1)} %get-tuple-element.78), channel_id=1, source_target_pairs={{0,0},{1,1},{2,2},{3,3},{4,4},{5,5},{6,6},{7,7},{8,8},{9,9},{10,10... | collective-permute-start | bytes 786440 | tf_op jit(solution)/shard_map/ppermute | solution.py:225
  41.6 11.5 %collective-permute-start.7 = (bf16[2,64,1024]{2,1,0:T(8,128)(2,1)S(1)}, bf16[2,64,1024]{2,1,0:T(8,128)(2,1)S(1)}, u32[]{:S(2)}, u32[]{:S(2)}) collective-permute-start(bf16[2,64,1024]{2,1,0:T(8,128)(2,1)S(1)} %get-tuple-element.78), channel_id=1, source_target_pairs={{0,0},{1,1},{2,2},{3,3},{4,4},{5,5},{6,6},{7,7},{8,8},{9,9},{10,10... | collective-permute-start | bytes 786440 | tf_op jit(solution)/shard_map/ppermute | solution.py:225
  43.5 12.3 %collective-permute-start.6 = (bf16[2,64,1024]{2,1,0:T(8,128)(2,1)S(1)}, bf16[2,64,1024]{2,1,0:T(8,128)(2,1)S(1)}, u32[]{:S(2)}, u32[]{:S(2)}) collective-permute-start(bf16[2,64,1024]{2,1,0:T(8,128)(2,1)S(1)} %get-tuple-element.78), channel_id=1, source_target_pairs={{0,0},{1,1},{2,2},{3,3},{4,4},{5,5},{6,6},{7,7},{8,8},{9,9},{10,10... | collective-permute-start | bytes 786440 | tf_op jit(solution)/shard_map/ppermute | solution.py:225
  48.5 9.9 %collective-permute-start.13 = (bf16[2,64,1024]{2,1,0:T(8,128)(2,1)S(1)}, bf16[2,64,1024]{2,1,0:T(8,128)(2,1)S(1)}, u32[]{:S(2)}, u32[]{:S(2)}) collective-permute-start(bf16[2,64,1024]{2,1,0:T(8,128)(2,1)S(1)} %get-tuple-element.148), channel_id=1, source_target_pairs={{0,31},{1,0},{2,1},{3,2},{4,3},{5,4},{6,5},{7,6},{8,7},{9,8},{10,9... | collective-permute-start | bytes 786440 | tf_op jit(solution)/shard_map/ppermute | solution.py:206
  50.5 7.9 %collective-permute-start.12 = (bf16[2,64,1024]{2,1,0:T(8,128)(2,1)S(1)}, bf16[2,64,1024]{2,1,0:T(8,128)(2,1)S(1)}, u32[]{:S(2)}, u32[]{:S(2)}) collective-permute-start(bf16[2,64,1024]{2,1,0:T(8,128)(2,1)S(1)} %get-tuple-element.148), channel_id=1, source_target_pairs={{0,1},{1,2},{2,3},{3,4},{4,5},{5,6},{6,7},{7,8},{8,9},{9,10},{10,1... | collective-permute-start | bytes 786440 | tf_op jit(solution)/shard_map/ppermute | solution.py:206
  56.4 2.1 collective-permute-start.11
  59.0 8.2 %collective-permute-start.16 = (bf16[2,64,1024]{2,1,0:T(8,128)(2,1)S(1)}, bf16[2,64,1024]{2,1,0:T(8,128)(2,1)S(1)}, u32[]{:S(2)}, u32[]{:S(2)}) collective-permute-start(bf16[2,64,1024]{2,1,0:T(8,128)(2,1)S(1)} %get-tuple-element.84), channel_id=1, source_target_pairs={{0,0},{1,32},{2,33},{3,34},{4,35},{5,36},{6,37},{7,38},{8,39},{9,4... | collective-permute-start | bytes 786440 | tf_op jit(solution)/shard_map/ppermute | solution.py:225
  61.0 9.8 %collective-permute-start.15 = (bf16[2,64,1024]{2,1,0:T(8,128)(2,1)S(1)}, bf16[2,64,1024]{2,1,0:T(8,128)(2,1)S(1)}, u32[]{:S(2)}, u32[]{:S(2)}) collective-permute-start(bf16[2,64,1024]{2,1,0:T(8,128)(2,1)S(1)} %get-tuple-element.84), channel_id=1, source_target_pairs={{0,33},{1,34},{2,35},{3,36},{4,37},{5,38},{6,39},{7,40},{8,41},{9,... | collective-permute-start | bytes 786440 | tf_op jit(solution)/shard_map/ppermute | solution.py:225
  64.8 6.0 %collective-permute-start.14 = (bf16[2,64,1024]{2,1,0:T(8,128)(2,1)S(1)}, bf16[2,64,1024]{2,1,0:T(8,128)(2,1)S(1)}, u32[]{:S(2)}, u32[]{:S(2)}) collective-permute-start(bf16[2,64,1024]{2,1,0:T(8,128)(2,1)S(1)} %get-tuple-element.84), channel_id=1, source_target_pairs={{0,32},{1,33},{2,34},{3,35},{4,36},{5,37},{6,38},{7,39},{8,40},{9,... | collective-permute-start | bytes 786440 | tf_op jit(solution)/shard_map/ppermute | solution.py:225
  73.5 14.1 %collective-permute-start.19 = (bf16[2,64,1024]{2,1,0:T(8,128)(2,1)S(1)}, bf16[2,64,1024]{2,1,0:T(8,128)(2,1)S(1)}, u32[]{:S(2)}, u32[]{:S(2)}) collective-permute-start(bf16[2,64,1024]{2,1,0:T(8,128)(2,1)S(1)} %get-tuple-element.87), channel_id=1, source_target_pairs={{0,0},{1,1},{2,2},{3,3},{4,4},{5,5},{6,6},{7,7},{8,8},{9,9},{10,10... | collective-permute-start | bytes 786440 | tf_op jit(solution)/shard_map/ppermute | solution.py:225
  78.8 9.9 %collective-permute-start.18 = (bf16[2,64,1024]{2,1,0:T(8,128)(2,1)S(1)}, bf16[2,64,1024]{2,1,0:T(8,128)(2,1)S(1)}, u32[]{:S(2)}, u32[]{:S(2)}) collective-permute-start(bf16[2,64,1024]{2,1,0:T(8,128)(2,1)S(1)} %get-tuple-element.87), channel_id=1, source_target_pairs={{0,0},{1,1},{2,2},{3,3},{4,4},{5,5},{6,6},{7,7},{8,8},{9,9},{10,10... | collective-permute-start | bytes 786440 | tf_op jit(solution)/shard_map/ppermute | solution.py:225
  80.7 10.7 %collective-permute-start.17 = (bf16[2,64,1024]{2,1,0:T(8,128)(2,1)S(1)}, bf16[2,64,1024]{2,1,0:T(8,128)(2,1)S(1)}, u32[]{:S(2)}, u32[]{:S(2)}) collective-permute-start(bf16[2,64,1024]{2,1,0:T(8,128)(2,1)S(1)} %get-tuple-element.87), channel_id=1, source_target_pairs={{0,0},{1,1},{2,2},{3,3},{4,4},{5,5},{6,6},{7,7},{8,8},{9,9},{10,10... | collective-permute-start | bytes 786440 | tf_op jit(solution)/shard_map/ppermute | solution.py:225
  92.0 2.1 collective-permute-start.22
  94.6 2.1 collective-permute-start.25
  110.8 125.7 %collective-permute-start.41 = (bf16[2,64,1024]{2,1,0:T(8,128)(2,1)S(1)}, bf16[2,64,1024]{2,1,0:T(8,128)(2,1)S(1)}, u32[]{:S(2)}, u32[]{:S(2)}) collective-permute-start(bf16[2,64,1024]{2,1,0:T(8,128)(2,1)S(1)} %get-tuple-element.121), channel_id=1, source_target_pairs={{0,0},{1,1},{2,2},{3,3},{4,4},{5,5},{6,6},{7,7},{8,8},{9,9},{10,10... | collective-permute-start | bytes 786440 | tf_op jit(solution)/shard_map/ppermute | solution.py:225
  231.4 8.6 %collective-permute-start.42 = (bf16[2,64,1024]{2,1,0:T(8,128)(2,1)S(1)}, bf16[2,64,1024]{2,1,0:T(8,128)(2,1)S(1)}, u32[]{:S(2)}, u32[]{:S(2)}) collective-permute-start(bf16[2,64,1024]{2,1,0:T(8,128)(2,1)S(1)} %get-tuple-element.122), channel_id=1, source_target_pairs={{0,0},{1,1},{2,2},{3,3},{4,4},{5,5},{6,6},{7,7},{8,8},{9,9},{10,10... | collective-permute-start | bytes 786440 | tf_op jit(solution)/shard_map/ppermute | solution.py:225
  233.4 10.7 %collective-permute-start.43 = (bf16[2,64,1024]{2,1,0:T(8,128)(2,1)S(1)}, bf16[2,64,1024]{2,1,0:T(8,128)(2,1)S(1)}, u32[]{:S(2)}, u32[]{:S(2)}) collective-permute-start(bf16[2,64,1024]{2,1,0:T(8,128)(2,1)S(1)} %get-tuple-element.123), channel_id=1, source_target_pairs={{0,0},{1,1},{2,2},{3,3},{4,4},{5,5},{6,6},{7,7},{8,8},{9,9},{10,10... | collective-permute-start | bytes 786440 | tf_op jit(solution)/shard_map/ppermute | solution.py:225
  246.3 8.3 %collective-permute-start.44 = (bf16[2,64,1024]{2,1,0:T(8,128)(2,1)S(1)}, bf16[2,64,1024]{2,1,0:T(8,128)(2,1)S(1)}, u32[]{:S(2)}, u32[]{:S(2)}) collective-permute-start(bf16[2,64,1024]{2,1,0:T(8,128)(2,1)S(1)} %get-tuple-element.126), channel_id=1, source_target_pairs={{0,32},{1,33},{2,34},{3,35},{4,36},{5,37},{6,38},{7,39},{8,40},{9,... | collective-permute-start | bytes 786440 | tf_op jit(solution)/shard_map/ppermute | solution.py:225
  248.2 11.2 %collective-permute-start.45 = (bf16[2,64,1024]{2,1,0:T(8,128)(2,1)S(1)}, bf16[2,64,1024]{2,1,0:T(8,128)(2,1)S(1)}, u32[]{:S(2)}, u32[]{:S(2)}) collective-permute-start(bf16[2,64,1024]{2,1,0:T(8,128)(2,1)S(1)} %get-tuple-element.127), channel_id=1, source_target_pairs={{0,33},{1,34},{2,35},{3,36},{4,37},{5,38},{6,39},{7,40},{8,41},{9,... | collective-permute-start | bytes 786440 | tf_op jit(solution)/shard_map/ppermute | solution.py:225
  252.6 8.0 %collective-permute-start.46 = (bf16[2,64,1024]{2,1,0:T(8,128)(2,1)S(1)}, bf16[2,64,1024]{2,1,0:T(8,128)(2,1)S(1)}, u32[]{:S(2)}, u32[]{:S(2)}) collective-permute-start(bf16[2,64,1024]{2,1,0:T(8,128)(2,1)S(1)} %get-tuple-element.128), channel_id=1, source_target_pairs={{0,0},{1,32},{2,33},{3,34},{4,35},{5,36},{6,37},{7,38},{8,39},{9,4... | collective-permute-start | bytes 786440 | tf_op jit(solution)/shard_map/ppermute | solution.py:225
  263.8 24.8 %collective-permute-start.50 = (bf16[2,64,1024]{2,1,0:T(8,128)(2,1)S(1)}, bf16[2,64,1024]{2,1,0:T(8,128)(2,1)S(1)}, u32[]{:S(2)}, u32[]{:S(2)}) collective-permute-start(bf16[2,64,1024]{2,1,0:T(8,128)(2,1)S(1)} %get-tuple-element.136), channel_id=1, source_target_pairs={{0,0},{1,1},{2,2},{3,3},{4,4},{5,5},{6,6},{7,7},{8,8},{9,9},{10,10... | collective-permute-start | bytes 786440 | tf_op jit(solution)/shard_map/ppermute | solution.py:225
  283.6 8.6 %collective-permute-start.51 = (bf16[2,64,1024]{2,1,0:T(8,128)(2,1)S(1)}, bf16[2,64,1024]{2,1,0:T(8,128)(2,1)S(1)}, u32[]{:S(2)}, u32[]{:S(2)}) collective-permute-start(bf16[2,64,1024]{2,1,0:T(8,128)(2,1)S(1)} %get-tuple-element.137), channel_id=1, source_target_pairs={{0,0},{1,1},{2,2},{3,3},{4,4},{5,5},{6,6},{7,7},{8,8},{9,9},{10,10... | collective-permute-start | bytes 786440 | tf_op jit(solution)/shard_map/ppermute | solution.py:225
  285.5 10.7 %collective-permute-start.52 = (bf16[2,64,1024]{2,1,0:T(8,128)(2,1)S(1)}, bf16[2,64,1024]{2,1,0:T(8,128)(2,1)S(1)}, u32[]{:S(2)}, u32[]{:S(2)}) collective-permute-start(bf16[2,64,1024]{2,1,0:T(8,128)(2,1)S(1)} %get-tuple-element.138), channel_id=1, source_target_pairs={{0,0},{1,1},{2,2},{3,3},{4,4},{5,5},{6,6},{7,7},{8,8},{9,9},{10,10... | collective-permute-start | bytes 786440 | tf_op jit(solution)/shard_map/ppermute | solution.py:225
  298.4 8.3 %collective-permute-start.53 = (bf16[2,64,1024]{2,1,0:T(8,128)(2,1)S(1)}, bf16[2,64,1024]{2,1,0:T(8,128)(2,1)S(1)}, u32[]{:S(2)}, u32[]{:S(2)}) collective-permute-start(bf16[2,64,1024]{2,1,0:T(8,128)(2,1)S(1)} %get-tuple-element.141), channel_id=1, source_target_pairs={{0,32},{1,33},{2,34},{3,35},{4,36},{5,37},{6,38},{7,39},{8,40},{9,... | collective-permute-start | bytes 786440 | tf_op jit(solution)/shard_map/ppermute | solution.py:225
  300.4 11.2 %collective-permute-start.54 = (bf16[2,64,1024]{2,1,0:T(8,128)(2,1)S(1)}, bf16[2,64,1024]{2,1,0:T(8,128)(2,1)S(1)}, u32[]{:S(2)}, u32[]{:S(2)}) collective-permute-start(bf16[2,64,1024]{2,1,0:T(8,128)(2,1)S(1)} %get-tuple-element.142), channel_id=1, source_target_pairs={{0,33},{1,34},{2,35},{3,36},{4,37},{5,38},{6,39},{7,40},{8,41},{9,... | collective-permute-start | bytes 786440 | tf_op jit(solution)/shard_map/ppermute | solution.py:225
  304.8 8.0 %collective-permute-start.55 = (bf16[2,64,1024]{2,1,0:T(8,128)(2,1)S(1)}, bf16[2,64,1024]{2,1,0:T(8,128)(2,1)S(1)}, u32[]{:S(2)}, u32[]{:S(2)}) collective-permute-start(bf16[2,64,1024]{2,1,0:T(8,128)(2,1)S(1)} %get-tuple-element.143), channel_id=1, source_target_pairs={{0,0},{1,32},{2,33},{3,34},{4,35},{5,36},{6,37},{7,38},{8,39},{9,4... | collective-permute-start | bytes 786440 | tf_op jit(solution)/shard_map/ppermute | solution.py:225
  (25 other events, 34.0 us)
